TPU v7x, 32 devices: a whole 2x2x4 slice. The times are simulated.
32 devices in a mesh: enc: 2 (over core), dp: 4 (over z), mp: 4 (over y, x).
Axes of the slice: x: 2, y: 2, z: 4, core: 2. Of those that a mesh axis runs over, the one named last changes fastest.
Arguments:
- token_ids: int32 [2, 16, 256], P('enc', 'dp'), may hold values from 0 to 30719
- query_lengths: int32 [32], P('dp'), may hold values from 1 to 128, 2048 in all
- negative_mask: int32 [32, 16], replicated, may hold values 0 or 1
- positive_index: int32 [32], replicated, may hold values from 0 to 15
- used_rows: int32 [32], replicated, may hold values 0 or 1
- step_count: int32 [1], replicated, may hold values from 2 to 20
- table: float32 [2, 30720, 768], P('enc', ('dp', 'mp')), may hold values from -0.18 to 0.18
- w_mixed: float32 [2, 768, 3, 768], P('enc', 'dp', None, 'mp'), may hold values from -0.21875 to 0.21875
- w_out: float32 [2, 768, 768], P('enc', 'mp', 'dp'), may hold values from -0.875 to 0.875
- w_inner: float32 [2, 768, 3072], P('enc', 'dp', 'mp'), may hold values from -0.21875 to 0.21875
- w_outer: float32 [2, 3072, 768], P('enc', 'mp', 'dp'), may hold values from -0.109375 to 0.109375
- norm_params: float32 [2, 6, 768], P('enc'), as said below
- table_m: float32 [2, 30720, 768], P('enc', ('dp', 'mp')), may hold values from -1.1234977e-06 to 1.1234977e-06
- table_v: float32 [2, 30720, 768], P('enc', ('dp', 'mp')), may hold values from 6.5198705e-15 to 2.6079482e-14
- mixed_m: float32 [2, 768, 3, 768], P('enc', 'dp', None, 'mp'), may hold values from -1.1234977e-06 to 1.1234977e-06
- mixed_v: float32 [2, 768, 3, 768], P('enc', 'dp', None, 'mp'), may hold values from 6.5198705e-15 to 2.6079482e-14
- out_m: float32 [2, 768, 768], P('enc', 'mp', 'dp'), may hold values from -1.1234977e-06 to 1.1234977e-06
- out_v: float32 [2, 768, 768], P('enc', 'mp', 'dp'), may hold values from 6.5198705e-15 to 2.6079482e-14
- inner_m: float32 [2, 768, 3072], P('enc', 'dp', 'mp'), may hold values from -1.1234977e-06 to 1.1234977e-06
- inner_v: float32 [2, 768, 3072], P('enc', 'dp', 'mp'), may hold values from 6.5198705e-15 to 2.6079482e-14
- outer_m: float32 [2, 3072, 768], P('enc', 'mp', 'dp'), may hold values from -1.1234977e-06 to 1.1234977e-06
- outer_v: float32 [2, 3072, 768], P('enc', 'mp', 'dp'), may hold values from 6.5198705e-15 to 2.6079482e-14
- norms_m: float32 [2, 6, 768], P('enc'), may hold values from -4.4684566e-06 to 4.4684566e-06
- norms_v: float32 [2, 6, 768], P('enc'), may hold values from 1.0431793e-13 to 4.172717e-13
Outputs:
- loss: float32 [], replicated
- grad_norm: float32 [], replicated
- table_new: float32 [2, 30720, 768], P('enc', ('dp', 'mp'))
- table_m_new: float32 [2, 30720, 768], P('enc', ('dp', 'mp'))
- table_v_new: float32 [2, 30720, 768], P('enc', ('dp', 'mp'))
- mixed_new: float32 [2, 768, 3, 768], P('enc', 'dp', None, 'mp')
- mixed_m_new: float32 [2, 768, 3, 768], P('enc', 'dp', None, 'mp')
- mixed_v_new: float32 [2, 768, 3, 768], P('enc', 'dp', None, 'mp')
- out_new: float32 [2, 768, 768], P('enc', 'mp', 'dp')
- out_m_new: float32 [2, 768, 768], P('enc', 'mp', 'dp')
- output_second_moment_next: float32 [2, 768, 768], P('enc', 'mp', 'dp')
- inner_new: float32 [2, 768, 3072], P('enc', 'dp', 'mp')
- inner_m_new: float32 [2, 768, 3072], P('enc', 'dp', 'mp')
- inner_v_new: float32 [2, 768, 3072], P('enc', 'dp', 'mp')
- outer_new: float32 [2, 3072, 768], P('enc', 'mp', 'dp')
- outer_m_new: float32 [2, 3072, 768], P('enc', 'mp', 'dp')
- outer_v_new: float32 [2, 3072, 768], P('enc', 'mp', 'dp')
- norms_new: float32 [2, 6, 768], P('enc')
- norms_m_new: float32 [2, 6, 768], P('enc')
- norms_v_new: float32 [2, 6, 768], P('enc')
Inputs may be any that keep to these rules, and one draw needn't show every extreme that they name: `norm_params`: gains (rows 0, 2, 4) lie in 0.7 to 1.3, shifts (rows 1, 3, 5) are small.
All inputs are finite; a program needn't handle non-finite values. No bound on the sum of `query_lengths` on one device may be relied on, other than what follows from the above.
Results may differ from a plain program's by a relative error of at most 0.015.
Values may be sent and summed in bfloat16 or wider, within the bound.
A program may use at most 192 MiB of HBM per device.

v0:
```python
from functools import partial
import jax
import jax.numpy as jnp
from jax import lax
from jax.sharding import PartitionSpec as P

D = 768
HEAD = 64
QSLOT = 128
SPANS = 2
exact_arithmetic_level = lax.Precision.HIGHEST
eps_norm = 1e-06
logit_divisor = 0.05
clip_limit = 0.02
beta_one = 0.9
beta_two = 0.999
adam_eps = 1e-08


def layer_norm(x, gain, shift):
    centred = x - jnp.mean(x, -1, keepdims=True)
    spread = jnp.mean(centred * centred, -1, keepdims=True)
    return centred * lax.rsqrt(spread + eps_norm) * gain + shift


def spread_rows(x):
    return lax.all_gather(x, "mp", axis=0, tiled=True)


def collect_rows(x):
    return lax.psum_scatter(x, "mp", scatter_dimension=0, tiled=True)


def contract_rows(left, right):
    return lax.dot_general(
        left, right, (((0,), (0,)), ((), ())), preferred_element_type=jnp.float32
    )


def contract_cols(left, right):
    return lax.dot_general(
        left, right, (((1,), (1,)), ((), ())), preferred_element_type=jnp.float32
    )


def vocab_place(flat_ids, table_rows):
    n_mp = lax.axis_size("mp")
    piece = table_rows // lax.axis_size("dp")
    block_num = flat_ids // piece
    local_row = block_num // n_mp * piece + flat_ids % piece
    owned = block_num % n_mp == lax.axis_index("mp")
    return (local_row, owned)


def attention_mask(lens_span, is_query, length):
    diagonal_indices = jnp.arange(length)
    segment = jnp.where(is_query, diagonal_indices // QSLOT, 0)
    limit = jnp.where(diagonal_indices[None, :] < QSLOT, lens_span[:, 0:1], lens_span[:, 1:2])
    key_ok = jnp.where(is_query, (diagonal_indices % QSLOT)[None, :] < limit, True)
    return (segment[:, None] == segment[None, :])[None] & key_ok[:, None, :]


def attention_scores(queries, keys, allowed):
    scores = jnp.einsum(
        "bqhd,bkhd->bhqk", queries, keys, preferred_element_type=jnp.float32
    ) * HEAD ** (-0.5)
    return jnp.where(allowed[:, None], scores, -1e30)


def forward_span(weights, norms, ids_span, allowed):
    table, w_mixed, w_out, w_inner, w_outer = weights
    blocks, length = ids_span.shape
    rows = blocks * length
    local_row, owned = vocab_place(ids_span.reshape(rows), table.shape[0])
    looked = jnp.where(owned[:, None], table[local_row].astype(jnp.float32), 0.0)
    embedded = lax.psum_scatter(
        looked.astype(jnp.bfloat16), "mp", scatter_dimension=0, tiled=True
    ).astype(jnp.float32)
    hidden0 = layer_norm(embedded, norms[0], norms[1])
    hid_all = spread_rows(hidden0.astype(jnp.bfloat16))
    mixed = jnp.dot(hid_all, w_mixed.reshape(D, -1), preferred_element_type=jnp.float32).astype(
        jnp.bfloat16
    )
    heads_local = w_out.shape[0] // HEAD
    parts = mixed.reshape(blocks, length, 3, heads_local, HEAD)
    scores = attention_scores(parts[:, :, 0], parts[:, :, 1], allowed)
    top = jnp.max(scores, -1, keepdims=True)
    log_total = top + jnp.log(jnp.sum(jnp.exp(scores - top), -1, keepdims=True))
    probs = jnp.exp(scores - log_total).astype(jnp.bfloat16)
    attended = jnp.einsum(
        "bhqk,bkhd->bqhd", probs, parts[:, :, 2], preferred_element_type=jnp.float32
    )
    attended = attended.astype(jnp.bfloat16).reshape(rows, -1)
    first_sum = hidden0 + collect_rows(jnp.dot(attended, w_out, preferred_element_type=jnp.float32))
    normed = layer_norm(first_sum, norms[2], norms[3])
    rescaled_everything = spread_rows(normed.astype(jnp.bfloat16))
    inner = jnp.dot(rescaled_everything, w_inner, preferred_element_type=jnp.float32)
    activated = jax.nn.gelu(inner, approximate=False).astype(jnp.bfloat16)
    second_sum = normed + collect_rows(
        jnp.dot(activated, w_outer, preferred_element_type=jnp.float32)
    )
    final = layer_norm(second_sum, norms[4], norms[5])
    saved = (
        embedded,
        hid_all,
        parts,
        log_total,
        attended,
        first_sum,
        rescaled_everything,
        inner,
        activated,
        second_sum,
    )
    return (final, saved)


def backward_span(weights, norms, ids_span, allowed, saved, grad_final):
    table, w_mixed, w_out, w_inner, w_outer = weights
    (
        embedded,
        hid_all,
        parts,
        log_total,
        attended,
        first_sum,
        rescaled_everything,
        inner,
        activated,
        second_sum,
    ) = saved
    blocks, length = ids_span.shape
    rows = blocks * length
    _, length_scaling_pullback = jax.vjp(layer_norm, second_sum, norms[4], norms[5])
    d_second, d_gain2, d_shift2 = length_scaling_pullback(grad_final)
    d_outer = spread_rows(d_second.astype(jnp.bfloat16))
    g_outer = contract_rows(activated, d_outer)
    d_act = contract_cols(d_outer, w_outer)
    _, gelu_back = jax.vjp(partial(jax.nn.gelu, approximate=False), inner)
    d_inner = gelu_back(d_act)[0].astype(jnp.bfloat16)
    g_inner = contract_rows(rescaled_everything, d_inner)
    d_normed = d_second + collect_rows(contract_cols(d_inner, w_inner))
    _, length_scaling_pullback = jax.vjp(layer_norm, first_sum, norms[2], norms[3])
    d_first, d_gain1, shift_gradient_middle = length_scaling_pullback(d_normed)
    d_attn = spread_rows(d_first.astype(jnp.bfloat16))
    g_out = contract_rows(attended, d_attn)
    d_attended = contract_cols(d_attn, w_out).astype(jnp.bfloat16).reshape(blocks, length, -1, HEAD)
    queries, keys, values = (parts[:, :, 0], parts[:, :, 1], parts[:, :, 2])
    probs = jnp.exp(attention_scores(queries, keys, allowed) - log_total)
    d_values = jnp.einsum(
        "bhqk,bqhd->bkhd",
        probs.astype(jnp.bfloat16),
        d_attended,
        preferred_element_type=jnp.float32,
    )
    d_probs = jnp.einsum("bqhd,bkhd->bhqk", d_attended, values, preferred_element_type=jnp.float32)
    d_scores = (probs * (d_probs - jnp.sum(probs * d_probs, -1, keepdims=True))).astype(
        jnp.bfloat16
    )
    d_queries = jnp.einsum(
        "bhqk,bkhd->bqhd", d_scores, keys, preferred_element_type=jnp.float32
    ) * HEAD ** (-0.5)
    d_keys = jnp.einsum(
        "bhqk,bqhd->bkhd", d_scores, queries, preferred_element_type=jnp.float32
    ) * HEAD ** (-0.5)
    d_mixed = jnp.stack([d_queries, d_keys, d_values], 2).astype(jnp.bfloat16).reshape(rows, -1)
    g_mixed = contract_rows(hid_all, d_mixed).reshape(w_mixed.shape)
    d_hidden = d_first + collect_rows(contract_cols(d_mixed, w_mixed.reshape(D, -1)))
    _, length_scaling_pullback = jax.vjp(layer_norm, embedded, norms[0], norms[1])
    d_embedded, d_gain0, d_shift0 = length_scaling_pullback(d_hidden)
    g_norms = jnp.stack([d_gain0, d_shift0, d_gain1, shift_gradient_middle, d_gain2, d_shift2])
    return ((g_mixed, g_out, g_inner, g_outer), d_embedded, g_norms)


def cls_picker(blocks, length):
    n_mp = lax.axis_size("mp")
    shard = blocks * length // n_mp
    global_row = lax.axis_index("mp") * shard + jnp.arange(shard)
    within = global_row % length
    slot = global_row // length * 2 + within // QSLOT
    hits = (slot[None, :] == jnp.arange(2 * blocks)[:, None]) & (within % QSLOT == 0)[None, :]
    return hits.astype(jnp.float32)


def contrast(queries, passages, negative_mask, positive_index, used_rows):
    question_direction_rows = queries * lax.rsqrt(
        jnp.sum(queries * queries, -1, keepdims=True) + eps_norm
    )
    document_direction_rows = passages * lax.rsqrt(
        jnp.sum(passages * passages, -1, keepdims=True) + eps_norm
    )
    pairwise_cosine_table = (
        jnp.dot(
            question_direction_rows, document_direction_rows.T, precision=exact_arithmetic_level
        )
        / logit_divisor
    )
    excluded = (negative_mask == 1) & (
        jnp.arange(passages.shape[0])[None, :] != positive_index[:, None]
    )
    pairwise_cosine_table = jnp.where(excluded, -1e30, pairwise_cosine_table)
    top = jnp.max(pairwise_cosine_table, -1, keepdims=True)
    log_total = top[:, 0] + jnp.log(jnp.sum(jnp.exp(pairwise_cosine_table - top), -1))
    target = jnp.take_along_axis(pairwise_cosine_table, positive_index[:, None], 1)[:, 0]
    weight = used_rows.astype(jnp.float32)
    return jnp.sum(weight * (log_total - target)) / jnp.maximum(jnp.sum(weight), 1.0)


def adam_step(weight, grad, first, second, rate, decay, count):
    first_new = beta_one * first + (1.0 - beta_one) * grad
    second_new = beta_two * second + (1.0 - beta_two) * grad * grad
    fix_one = 1.0 - jnp.power(beta_one, count)
    correction_second = 1.0 - jnp.power(beta_two, count)
    update = (
        first_new / fix_one / (jnp.sqrt(second_new / correction_second) + adam_eps) + decay * weight
    )
    return (weight - rate * update, first_new, second_new)


def on_device(
    token_ids,
    query_lengths,
    negative_mask,
    positive_index,
    used_rows,
    step_count,
    table,
    w_mixed,
    w_out,
    w_inner,
    w_outer,
    norm_params,
    table_m,
    table_v,
    mixed_m,
    mixed_v,
    out_m,
    out_v,
    inner_m,
    inner_v,
    outer_m,
    outer_v,
    norms_m,
    norms_v,
):
    is_query = lax.axis_index("enc") == 0
    gathered = (
        lax.all_gather(table.astype(jnp.bfloat16), "dp", axis=1, tiled=True),
        lax.all_gather(w_mixed.astype(jnp.bfloat16), "dp", axis=1, tiled=True),
        lax.all_gather(w_out.astype(jnp.bfloat16), "dp", axis=2, tiled=True),
        lax.all_gather(w_inner.astype(jnp.bfloat16), "dp", axis=1, tiled=True),
        lax.all_gather(w_outer.astype(jnp.bfloat16), "dp", axis=2, tiled=True),
    )
    weights = tuple((item[0] for item in gathered))
    norms = norm_params[0]
    ids_all = token_ids[0]
    blk, length = ids_all.shape
    per_span = blk // SPANS
    lens_all = query_lengths.reshape(blk, 2)
    picker = cls_picker(per_span, length)
    masks, saved_list, cls_parts = ([], [], [])
    for index in range(SPANS):
        ids_span = ids_all[index * per_span : (index + 1) * per_span]
        allowed = attention_mask(
            lens_all[index * per_span : (index + 1) * per_span], is_query, length
        )
        final, saved = forward_span(weights, norms, ids_span, allowed)
        cls_parts.append(jnp.dot(picker, final, precision=exact_arithmetic_level))
        masks.append(allowed)
        saved_list.append(saved)
    cls_mine = lax.psum(jnp.concatenate(cls_parts, 0), "mp")
    cls_all = lax.all_gather(cls_mine, ("enc", "dp"), axis=0, tiled=True)
    n_dp = lax.axis_size("dp")
    cls_all = cls_all.reshape(2, n_dp * 2 * blk, D)
    queries = cls_all[0]
    passages = cls_all[1, 0::2]
    loss, loss_back = jax.vjp(
        partial(
            contrast,
            negative_mask=negative_mask,
            positive_index=positive_index,
            used_rows=used_rows,
        ),
        queries,
        passages,
    )
    d_queries, d_passages = loss_back(jnp.ones((), jnp.float32))
    d_pass_full = jnp.zeros_like(queries).at[0::2].set(d_passages)
    d_cls = jnp.where(is_query, d_queries, d_pass_full)
    d_mine = lax.dynamic_slice_in_dim(d_cls, lax.axis_index("dp") * 2 * blk, 2 * blk, 0)
    totals = None
    g_norms = jnp.zeros((6, D), jnp.float32)
    for index in range(SPANS):
        ids_span = ids_all[index * per_span : (index + 1) * per_span]
        _, saved = forward_span(weights, norms, ids_span, masks[index])
        grad_final = lax.dot_general(
            picker,
            d_mine[index * 2 * per_span : (index + 1) * 2 * per_span],
            (((0,), (0,)), ((), ())),
            precision=exact_arithmetic_level,
            preferred_element_type=jnp.float32,
        )
        mats, d_embedded, span_norms = backward_span(
            weights, norms, ids_span, masks[index], saved, grad_final
        )
        g_norms = g_norms + span_norms
        flat_ids = ids_span.reshape(-1)
        d_rows = lax.all_gather(d_embedded, "mp", axis=0, tiled=True)
        local_row, owned = vocab_place(flat_ids, weights[0].shape[0])
        g_table = (
            jnp.zeros(weights[0].shape, jnp.float32)
            .at[local_row]
            .add(jnp.where(owned[:, None], d_rows, 0.0))
        )
        span_grads = (g_table,) + mats
        totals = (
            span_grads if totals is None else tuple((a + b for a, b in zip(totals, span_grads)))
        )
    shards = (
        lax.psum_scatter(totals[0][None], "dp", scatter_dimension=1, tiled=True),
        lax.psum_scatter(totals[1][None], "dp", scatter_dimension=1, tiled=True),
        lax.psum_scatter(totals[2][None], "dp", scatter_dimension=2, tiled=True),
        lax.psum_scatter(totals[3][None], "dp", scatter_dimension=1, tiled=True),
        lax.psum_scatter(totals[4][None], "dp", scatter_dimension=2, tiled=True),
    )
    g_norms = lax.psum(g_norms, ("dp", "mp"))
    owner = (lax.axis_index("dp") == 0) & (lax.axis_index("mp") == 0)
    squares = jnp.where(owner, jnp.sum(g_norms * g_norms), 0.0)
    for shard in shards:
        squares = squares + jnp.sum(shard * shard)
    grad_norm = jnp.sqrt(lax.psum(squares, ("enc", "dp", "mp")))
    clip = jnp.minimum(1.0, clip_limit / (grad_norm + 1e-06))
    count = step_count[0].astype(jnp.float32)
    masters = (table, w_mixed, w_out, w_inner, w_outer)
    firsts = (table_m, mixed_m, out_m, inner_m, outer_m)
    seconds = (table_v, mixed_v, out_v, inner_v, outer_v)
    results = []
    for index in range(5):
        results.append(
            adam_step(
                masters[index],
                shards[index] * clip,
                firsts[index],
                seconds[index],
                0.06,
                0.01,
                count,
            )
        )
    results.append(adam_step(norm_params, g_norms[None] * clip, norms_m, norms_v, 0.5, 0.0, count))
    return (
        loss,
        grad_norm,
        results[0][0],
        results[0][1],
        results[0][2],
        results[1][0],
        results[1][1],
        results[1][2],
        results[2][0],
        results[2][1],
        results[2][2],
        results[3][0],
        results[3][1],
        results[3][2],
        results[4][0],
        results[4][1],
        results[4][2],
        results[5][0],
        results[5][1],
        results[5][2],
    )


def solution(mesh):
    placed = (
        P("enc", "dp", None),
        P("dp"),
        P(),
        P(),
        P(),
        P(),
        P("enc", ("dp", "mp"), None),
        P("enc", "dp", None, "mp"),
        P("enc", "mp", "dp"),
        P("enc", "dp", "mp"),
        P("enc", "mp", "dp"),
        P("enc", None, None),
        P("enc", ("dp", "mp"), None),
        P("enc", ("dp", "mp"), None),
        P("enc", "dp", None, "mp"),
        P("enc", "dp", None, "mp"),
        P("enc", "mp", "dp"),
        P("enc", "mp", "dp"),
        P("enc", "dp", "mp"),
        P("enc", "dp", "mp"),
        P("enc", "mp", "dp"),
        P("enc", "mp", "dp"),
        P("enc", None, None),
        P("enc", None, None),
    )
    return jax.shard_map(
        on_device,
        mesh=mesh,
        in_specs=placed,
        out_specs=(
            P(),
            P(),
            P("enc", ("dp", "mp"), None),
            P("enc", ("dp", "mp"), None),
            P("enc", ("dp", "mp"), None),
            P("enc", "dp", None, "mp"),
            P("enc", "dp", None, "mp"),
            P("enc", "dp", None, "mp"),
            P("enc", "mp", "dp"),
            P("enc", "mp", "dp"),
            P("enc", "mp", "dp"),
            P("enc", "dp", "mp"),
            P("enc", "dp", "mp"),
            P("enc", "dp", "mp"),
            P("enc", "mp", "dp"),
            P("enc", "mp", "dp"),
            P("enc", "mp", "dp"),
            P("enc", None, None),
            P("enc", None, None),
            P("enc", None, None),
        ),
        check_vma=False,
    )
```

profile of v0, /device:TPU:0, one launch (start us, length us, event | category | flops | bytes accessed | tf_op | source)
XLA Modules:
  0.0 1548.0 jit_solution(6013270489068151891)
XLA Ops:
  7.2 4.6 convert_element_type.165
  13.2 50.5 %all_gather.54 = bf16[1,768,3,192]{3,2,0,1:T(4,128)(2,1)S(1)} all-gather(bf16[1,192,3,192]{3,2,0,1:T(4,128)(2,1)S(1)} %copy.212), channel_id=1, replica_groups=mesh['enc'=2,'dp'=4,'mp'=4] {'dp'}, dimensions={1}, use_global_device_ids=true | all-gather | bytes 1105920 | tf_op jit(solution)/shard_map/all_gather | solution.py:249
  65.0 32.1 %all_gather.55 = bf16[1,192,768]{1,0,2:T(2,128)(2,1)S(1)} all-gather(bf16[1,192,192]{1,0,2:T(2,128)(2,1)S(1)} %copy.219), channel_id=1, replica_groups=mesh['enc'=2,'dp'=4,'mp'=4] {'dp'}, dimensions={2}, use_global_device_ids=true | all-gather | bytes 368640 | tf_op jit(solution)/shard_map/all_gather | solution.py:250
  97.7 150.2 %all-gather.6.cloned.1.call-done = bf16[1,7680,768]{2,1,0:T(8,128)(2,1)} async-done(((bf16[1,1920,768]{2,1,0:T(8,128)(2,1)}), bf16[1,7680,768]{2,1,0:T(8,128)(2,1)}) %all-gather.6.cloned.1.call-update) | async-done | bytes 11796496 | tf_op jit(solution)/shard_map/all_gather | solution.py:248
  248.0 8.3 gather_fusion
  259.4 8.4 gather_fusion.1
  268.9 14.0 reduce-scatter.19.cloned.1.call-done
  286.3 14.5 all_gather.53
  309.4 4.0 reduce-scatter.25.cloned.1.call-done
  316.2 31.6 %reduce-scatter.21.cloned.1.call-done = f32[128,768]{1,0:T(8,128)} async-done(((f32[512,768]{1,0:T(8,128)}), f32[128,768]{1,0:T(8,128)}) %reduce-scatter.21.cloned.1.call-update) | async-done | bytes 393232 | tf_op jit(solution)/shard_map/reduce_scatter | solution.py:31
  349.6 11.3 all_gather.59
  372.4 11.2 all_gather.56
  383.6 7.2 multiply_convert_fusion.3
  390.9 20.9 %all-gather.10.cloned.1.call-done = bf16[1,768,768]{1,2,0:T(8,128)(2,1)} async-done(((bf16[1,768,192]{1,2,0:T(8,128)(2,1)}), bf16[1,768,768]{1,2,0:T(8,128)(2,1)}) %all-gather.10.cloned.1.call-update) | async-done | bytes 1179664 | tf_op jit(solution)/shard_map/all_gather | solution.py:252
  411.8 3.5 fusion.31
  415.3 29.5 %reduce-scatter.27.cloned.1.call-done = f32[128,768]{1,0:T(8,128)} async-done(((f32[512,768]{1,0:T(8,128)}), f32[128,768]{1,0:T(8,128)}) %reduce-scatter.27.cloned.1.call-update) | async-done | bytes 393232 | tf_op jit(solution)/shard_map/reduce_scatter | solution.py:31
  448.0 31.4 %reduce-scatter.23.cloned.1.call-done = f32[128,768]{1,0:T(8,128)} async-done(((f32[512,768]{1,0:T(8,128)}), f32[128,768]{1,0:T(8,128)}) %reduce-scatter.23.cloned.1.call-update) | async-done | bytes 393232 | tf_op jit(solution)/shard_map/reduce_scatter | solution.py:31
  479.4 2.6 fusion.179
  482.0 11.1 all_gather.60
  493.1 5.3 multiply_convert_fusion.2
  509.2 23.3 %reduce-scatter.29.cloned.1.call-done = f32[128,768]{1,0:T(8,128)} async-done(((f32[512,768]{1,0:T(8,128)}), f32[128,768]{1,0:T(8,128)}) %reduce-scatter.29.cloned.1.call-update) | async-done | bytes 393232 | tf_op jit(solution)/shard_map/reduce_scatter | solution.py:31
  535.7 16.5 %psum.21 = f32[8,768]{1,0:T(8,128)} all-reduce(f32[8,768]{1,0:T(8,128)} %pad_maximum_fusion), channel_id=1, replica_groups=mesh['enc'=2,'dp'=4,'mp'=4] {'mp'}, use_global_device_ids=true, to_apply=%region_22.23 | all-reduce | flops 6144 | bytes 49152 | tf_op jit(solution)/shard_map/psum | solution.py:271
  552.3 24.7 %all_gather.61 = f32[64,768]{1,0:T(8,128)S(1)} all-gather(f32[8,768]{1,0:T(8,128)} %psum.21), channel_id=1, replica_groups=mesh['enc'=2,'dp'=4,'mp'=4] {'enc','dp'}, dimensions={0}, use_global_device_ids=true | all-gather | bytes 221184 | tf_op jit(solution)/shard_map/all_gather | solution.py:272
  605.6 12.2 all_gather.64
  623.6 15.7 %all_gather.62 = bf16[512,768]{1,0:T(8,128)(2,1)S(1)} all-gather(bf16[128,768]{1,0:T(8,128)(2,1)S(1)} %add_convert_fusion.5), channel_id=1, replica_groups=mesh['enc'=2,'dp'=4,'mp'=4] {'mp'}, dimensions={0}, use_global_device_ids=true | all-gather | bytes 983040 | tf_op jit(solution)/shard_map/all_gather | solution.py:27
  639.3 3.3 add_convert_fusion.1
  645.6 8.6 reduce-scatter.35.cloned.1.call-done
  654.1 34.5 %reduce-scatter.31.cloned.1.call-done = f32[128,768]{1,0:T(8,128)} async-done(((f32[512,768]{1,0:T(8,128)}), f32[128,768]{1,0:T(8,128)}) %reduce-scatter.31.cloned.1.call-update) | async-done | bytes 393232 | tf_op jit(solution)/shard_map/reduce_scatter | solution.py:31
  695.6 11.1 all_gather.63
  716.6 14.9 all_gather.65
  739.8 9.0 reduce-scatter.33.cloned.1.call-done
  748.9 34.5 %reduce-scatter.37.cloned.1.call-done = f32[128,768]{1,0:T(8,128)} async-done(((f32[512,768]{1,0:T(8,128)}), f32[128,768]{1,0:T(8,128)}) %reduce-scatter.37.cloned.1.call-update) | async-done | bytes 393232 | tf_op jit(solution)/shard_map/reduce_scatter | solution.py:31
  790.7 4.3 copy.238
  808.1 2.9 copy.258
  811.0 2.8 reshape.1031
  814.5 3.7 all-gather.12.cloned.1.call-done
  819.8 31.7 %all-gather.14.cloned.1.call-done = f32[512,768]{1,0:T(8,128)} async-done(((f32[128,768]{1,0:T(8,128)}), f32[512,768]{1,0:T(8,128)}) %all-gather.14.cloned.1.call-update) | async-done | bytes 1572880 | tf_op jit(solution)/shard_map/all_gather | solution.py:308
  853.1 16.9 %scatter_custom_fusion.1 = f32[7680,768]{1,0:T(8,128)} fusion(s32[1024]{0:T(1024)S(1)} %bitcast.302, f32[]{:T(128)} %constant.335.clone.1, f32[512,768]{1,0:T(8,128)S(1)} %broadcast_select_fusion, f32[]{:T(128)} %constant.342.clone.1, f32[512,768]{1,0:T(8,128)S(1)} %broadcast_select_fusion.1), kind=kCustom, calls=%fused_computation.5 | custom fusion | flops 1572864 | bytes 26738696 | tf_op jit(solution)/shard_map/add | solution.py:317
  875.1 74.9 %all-reduce.3.cloned.1.call-done = f32[1,768,768]{1,0,2:T(1,128)} async-done(((f32[1,768,768]{1,0,2:T(1,128)}), f32[1,768,768]{1,0,2:T(1,128)}) %all-reduce.3.cloned.1.call-update) | async-done | bytes 2359312
  950.0 3.6 multiply_reduce_fusion.3
  953.7 20.8 %reduce-scatter.45.cloned.1.call-done = f32[192,192]{1,0:T(8,128)} async-done(((f32[768,192]{1,0:T(8,128)}), f32[192,192]{1,0:T(8,128)}) %reduce-scatter.45.cloned.1.call-update) | async-done | bytes 147472
  976.3 48.2 %reduce-scatter.41.cloned.1.call-done = f32[1,192,768]{2,1,0:T(8,128)} async-done(((f32[1,768,768]{2,1,0:T(8,128)}), f32[1,192,768]{2,1,0:T(8,128)}) %reduce-scatter.41.cloned.1.call-update) | async-done | bytes 589840 | tf_op jit(solution)/shard_map/reduce_scatter | solution.py:323
  1026.5 77.3 %psum.22 = f32[6,768]{1,0:T(8,128)S(1)} all-reduce(f32[6,768]{1,0:T(8,128)S(1)} %add.660), channel_id=1, replica_groups=mesh['enc'=2,'dp'=4,'mp'=4] {'dp','mp'}, use_global_device_ids=true, to_apply=%region_60.61 | all-reduce | flops 4608 | bytes 36864 | tf_op jit(solution)/shard_map/psum | solution.py:326
  1107.5 352.3 %reduce-scatter.39.cloned.1.call-done = f32[1,1920,768]{2,1,0:T(8,128)} async-done(((f32[1,7680,768]{2,1,0:T(8,128)}), f32[1,1920,768]{2,1,0:T(8,128)}) %reduce-scatter.39.cloned.1.call-update) | async-done | bytes 5898256 | tf_op jit(solution)/shard_map/reduce_scatter | solution.py:320
  1459.8 4.8 multiply_reduce_fusion
  1468.4 42.6 %psum.23 = f32[]{:T(128)} all-reduce(f32[]{:T(128)S(6)} %add.670), channel_id=1, replica_groups=mesh['enc'=2,'dp'=4,'mp'=4] {'enc','dp','mp'}, use_global_device_ids=true, to_apply=%region_77.78 | all-reduce | flops 1 | bytes 8 | tf_op jit(solution)/shard_map/psum | solution.py:331
  1521.5 2.9 multiply_subtract_fusion.1
  1525.9 12.6 multiply_subtract_fusion
  (584 shorter events, 158.7 us)
Async XLA Ops:
  7.2 240.8 %all-gather.6.cloned.1.call-start = ((), (), s32[]{:S(2)}) async-start(), calls=%async_computation.14 | async-start | bytes 14745600 | tf_op jit(solution)/shard_map/all_gather | solution.py:248
  11.8 271.1 %reduce-scatter.19.cloned.1.call-start = ((), (), s32[]{:S(2)}) async-start(), calls=%async_computation.15 | async-start | bytes 983040 | tf_op jit(solution)/shard_map/reduce_scatter | solution.py:76
  64.5 296.3 %copy-start.8 = (bf16[1,768,3,192]{1,3,2,0:T(8,128)(2,1)}, bf16[1,768,3,192]{1,3,2,0:T(8,128)(2,1)S(1)}, u32[]{:S(2)}) copy-start(bf16[1,768,3,192]{1,3,2,0:T(8,128)(2,1)S(1)} %copy.213) | copy-start | bytes 2654212
  97.6 207.4 %copy-start.10 = (bf16[1,192,768]{2,1,0:T(8,128)(2,1)}, bf16[1,192,768]{2,1,0:T(8,128)(2,1)S(1)}, u32[]{:S(2)}) copy-start(bf16[1,192,768]{2,1,0:T(8,128)(2,1)S(1)} %copy.220) | copy-start | bytes 884740
  97.7 158.6 %copy-start.89 = (s32[512,1]{0,1:T(1,128)}, s32[512,1]{0,1:T(1,128)S(1)}, u32[]{:S(2)}) copy-start(s32[512,1]{0,1:T(1,128)S(1)} %get-tuple-element.262) | copy-start | bytes 6148
  97.7 159.8 %copy-start.87 = (s32[512,1]{0,1:T(1,128)}, s32[512,1]{0,1:T(1,128)S(1)}, u32[]{:S(2)}) copy-start(s32[512,1]{0,1:T(1,128)S(1)} %get-tuple-element.261) | copy-start | bytes 6148
  97.7 158.5 %copy-start.126 = (pred[512]{0:T(512)(128)(4,1)}, pred[512]{0:T(512)(128)(4,1)S(1)}, u32[]{:S(2)}) copy-start(pred[512]{0:T(512)(128)(4,1)S(1)} %fusion.142) | copy-start | bytes 1540
  257.4 56.0 %reduce-scatter.25.cloned.1.call-start = ((), (), s32[]{:S(2)}) async-start(), calls=%async_computation.20 | async-start | bytes 983040 | tf_op jit(solution)/shard_map/reduce_scatter | solution.py:76
  258.3 221.1 %copy-start.81 = (f32[768]{0:T(1024)}, f32[768]{0:T(1024)S(1)}, u32[]{:S(2)}) copy-start(f32[768]{0:T(1024)S(1)} %get-tuple-element.139) | copy-start | bytes 9220
  258.3 274.1 %copy-start.75 = (f32[768]{0:T(1024)}, f32[768]{0:T(1024)S(1)}, u32[]{:S(2)}) copy-start(f32[768]{0:T(1024)S(1)} %get-tuple-element.140) | copy-start | bytes 9220
  258.3 276.2 %copy-start.77 = (f32[768]{0:T(1024)}, f32[768]{0:T(1024)S(1)}, u32[]{:S(2)}) copy-start(f32[768]{0:T(1024)S(1)} %get-tuple-element.138) | copy-start | bytes 9220
  268.9 78.8 %reduce-scatter.21.cloned.1.call-start = ((), (), s32[]{:S(2)}) async-start(), calls=%async_computation.16 | async-start | bytes 1966080 | tf_op jit(solution)/shard_map/reduce_scatter | solution.py:31
  306.5 77.1 %all-gather.8.cloned.1.call-start = ((), (), s32[]{:S(2)}) async-start(), calls=%async_computation.17 | async-start | bytes 1474560 | tf_op jit(solution)/shard_map/all_gather | solution.py:251
  308.5 103.3 %all-gather.10.cloned.1.call-start = ((), (), s32[]{:S(2)}) async-start(), calls=%async_computation.18 | async-start | bytes 1474560 | tf_op jit(solution)/shard_map/all_gather | solution.py:252
  309.3 135.5 %reduce-scatter.27.cloned.1.call-start = ((), (), s32[]{:S(2)}) async-start(), calls=%async_computation.21 | async-start | bytes 1966080 | tf_op jit(solution)/shard_map/reduce_scatter | solution.py:31
  314.4 48.8 %copy-start.93 = (f32[128]{0:T(128)}, f32[128]{0:T(128)S(1)}, u32[]{:S(2)}) copy-start(f32[128]{0:T(128)S(1)} %broadcast_multiply_fusion.2) | copy-start | bytes 1540
  316.2 47.1 %copy-start.119 = (f32[128]{0:T(128)}, f32[128]{0:T(128)S(1)}, u32[]{:S(2)}) copy-start(f32[128]{0:T(128)S(1)} %fusion.156) | copy-start | bytes 1540
  370.9 108.5 %reduce-scatter.23.cloned.1.call-start = ((), (), s32[]{:S(2)}) async-start(), calls=%async_computation.19 | async-start | bytes 1966080 | tf_op jit(solution)/shard_map/reduce_scatter | solution.py:31
  415.3 117.2 %reduce-scatter.29.cloned.1.call-start = ((), (), s32[]{:S(2)}) async-start(), calls=%async_computation.22 | async-start | bytes 1966080 | tf_op jit(solution)/shard_map/reduce_scatter | solution.py:31
  501.4 152.8 %reduce-scatter.35.cloned.1.call-start = ((), (), s32[]{:S(2)}) async-start(), calls=%async_computation.25 | async-start | bytes 1966080 | tf_op jit(solution)/shard_map/reduce_scatter | solution.py:31
  533.7 46.5 %copy-start.115 = (f32[128]{0:T(128)}, f32[128]{0:T(128)S(1)}, u32[]{:S(2)}) copy-start(f32[128]{0:T(128)S(1)} %broadcast_multiply_fusion) | copy-start | bytes 1540
  621.9 66.8 %reduce-scatter.31.cloned.1.call-start = ((), (), s32[]{:S(2)}) async-start(), calls=%async_computation.23 | async-start | bytes 1966080 | tf_op jit(solution)/shard_map/reduce_scatter | solution.py:31
  645.5 103.4 %reduce-scatter.33.cloned.1.call-start = ((), (), s32[]{:S(2)}) async-start(), calls=%async_computation.24 | async-start | bytes 1966080 | tf_op jit(solution)/shard_map/reduce_scatter | solution.py:31
  715.8 67.6 %reduce-scatter.37.cloned.1.call-start = ((), (), s32[]{:S(2)}) async-start(), calls=%async_computation.26 | async-start | bytes 1966080 | tf_op jit(solution)/shard_map/reduce_scatter | solution.py:31
  737.7 45.7 %copy-start.6 = (bf16[128,768]{1,0:T(8,128)(2,1)S(1)}, bf16[128,768]{1,0:T(8,128)(2,1)}, u32[]{:S(2)}) copy-start(bf16[128,768]{1,0:T(8,128)(2,1)} %reduce-scatter.19.cloned.1.call-done) | copy-start | bytes 589828
  737.7 45.7 %copy-start.7 = (bf16[128,768]{1,0:T(8,128)(2,1)S(1)}, bf16[128,768]{1,0:T(8,128)(2,1)}, u32[]{:S(2)}) copy-start(bf16[128,768]{1,0:T(8,128)(2,1)} %reduce-scatter.25.cloned.1.call-done) | copy-start | bytes 589828
  737.7 45.7 %copy-start.23 = (f32[128,768]{1,0:T(8,128)S(1)}, f32[128,768]{1,0:T(8,128)}, u32[]{:S(2)}) copy-start(f32[128,768]{1,0:T(8,128)} %copy-done.22) | copy-start | bytes 1179652
  737.7 45.6 %copy-start.92 = (f32[128]{0:T(128)S(1)}, f32[128]{0:T(128)}, u32[]{:S(2)}) copy-start(f32[128]{0:T(128)} %copy-done.91) | copy-start | bytes 1540
  737.7 45.6 %copy-start.94 = (f32[128]{0:T(128)S(1)}, f32[128]{0:T(128)}, u32[]{:S(2)}) copy-start(f32[128]{0:T(128)} %copy-done.93) | copy-start | bytes 1540
  737.7 45.6 %copy-start.134 = (f32[128]{0:T(128)S(1)}, f32[128]{0:T(128)}, u32[]{:S(2)}) copy-start(f32[128]{0:T(128)} %copy-done.133) | copy-start | bytes 1540
  737.8 45.6 %copy-start.136 = (f32[128]{0:T(128)S(1)}, f32[128]{0:T(128)}, u32[]{:S(2)}) copy-start(f32[128]{0:T(128)} %copy-done.135) | copy-start | bytes 1540
  739.8 45.1 %copy-start.118 = (f32[128]{0:T(128)S(1)}, f32[128]{0:T(128)}, u32[]{:S(2)}) copy-start(f32[128]{0:T(128)} %copy-done.117) | copy-start | bytes 1540
  739.8 78.5 %all-gather.12.cloned.1.call-start = ((), (), s32[]{:S(2)}) async-start(), calls=%async_computation.27 | async-start | bytes 1966080 | tf_op jit(solution)/shard_map/all_gather | solution.py:308
  787.1 64.4 %all-gather.14.cloned.1.call-start = ((), (), s32[]{:S(2)}) async-start(), calls=%async_computation.28 | async-start | bytes 1966080 | tf_op jit(solution)/shard_map/all_gather | solution.py:308
  787.7 162.3 %all-reduce.3.cloned.1.call-start = ((), (), s32[]{:S(2)}) async-start(), calls=%async_computation.33 | async-start | bytes 4718592
  795.0 179.4 %reduce-scatter.45.cloned.1.call-start = ((), (), s32[]{:S(2)}) async-start(), calls=%async_computation.32 | async-start | bytes 983040
  799.4 225.1 %reduce-scatter.41.cloned.1.call-start = ((), (), s32[]{:S(2)}) async-start(), calls=%async_computation.30 | async-start | bytes 2949120 | tf_op jit(solution)/shard_map/reduce_scatter | solution.py:323
  803.8 301.3 %reduce-scatter.43.cloned.1.call-start = ((), (), s32[]{:S(2)}) async-start(), calls=%async_computation.31 | async-start | bytes 2457600
  813.8 645.9 %reduce-scatter.39.cloned.1.call-start = ((), (), s32[]{:S(2)}) async-start(), calls=%async_computation.29 | async-start | bytes 29491200 | tf_op jit(solution)/shard_map/reduce_scatter | solution.py:320
  872.1 81.5 %copy-start.101 = (f32[768]{0:T(1024)S(1)}, f32[768]{0:T(1024)}, u32[]{:S(2)}) copy-start(f32[768]{0:T(1024)} %get-tuple-element.219) | copy-start | bytes 9220
  872.1 81.5 %copy-start.100 = (f32[768]{0:T(1024)S(1)}, f32[768]{0:T(1024)}, u32[]{:S(2)}) copy-start(f32[768]{0:T(1024)} %get-tuple-element.217) | copy-start | bytes 9220
  872.1 81.5 %copy-start.99 = (f32[768]{0:T(1024)S(1)}, f32[768]{0:T(1024)}, u32[]{:S(2)}) copy-start(f32[768]{0:T(1024)} %get-tuple-element.126) | copy-start | bytes 9220
  873.7 152.6 %copy-start.105 = (f32[768]{0:T(1024)S(1)}, f32[768]{0:T(1024)}, u32[]{:S(2)}) copy-start(f32[768]{0:T(1024)} %get-tuple-element.147) | copy-start | bytes 9220
  873.7 152.6 %copy-start.104 = (f32[768]{0:T(1024)S(1)}, f32[768]{0:T(1024)}, u32[]{:S(2)}) copy-start(f32[768]{0:T(1024)} %get-tuple-element.146) | copy-start | bytes 9220
  873.7 152.6 %copy-start.103 = (f32[768]{0:T(1024)S(1)}, f32[768]{0:T(1024)}, u32[]{:S(2)}) copy-start(f32[768]{0:T(1024)} %get-tuple-element.129) | copy-start | bytes 9220
  873.8 152.7 %copy-start.102 = (f32[768]{0:T(1024)S(1)}, f32[768]{0:T(1024)}, u32[]{:S(2)}) copy-start(f32[768]{0:T(1024)} %get-tuple-element.132) | copy-start | bytes 9220
  975.7 130.8 %copy-start.45 = (f32[1,192,192]{2,1,0:T(8,128)}, f32[1,192,192]{2,1,0:T(8,128)S(1)}, u32[]{:S(2)}) copy-start(f32[1,192,192]{2,1,0:T(8,128)S(1)} %copy.261) | copy-start | bytes 442372
  1107.5 404.3 %copy-start.86 = (f32[1,6,768]{2,0,1:T(1,128)S(1)}, f32[1,6,768]{2,0,1:T(1,128)}, u32[]{:S(2)}) copy-start(f32[1,6,768]{2,0,1:T(1,128)} %param.46) | copy-start | bytes 55300
  (136 other events, 899.2 us)
Sparse Core Ops, SparseCore 0:
  11.9 235.9 all-gather.5
  257.5 25.3 reduce-scatter.18
  286.4 26.9 reduce-scatter.24
  316.8 30.8 reduce-scatter.20
  349.7 30.4 all-gather.7
  382.2 29.5 all-gather.9
  414.8 30.0 reduce-scatter.26
  448.4 30.9 reduce-scatter.22
  501.5 30.9 reduce-scatter.28
  622.0 32.0 reduce-scatter.34
  657.7 30.8 reduce-scatter.30
  715.9 32.9 reduce-scatter.32
  752.4 30.8 reduce-scatter.36
  787.2 30.9 all-gather.11
  820.5 30.9 all-gather.13
  854.3 95.6 all-reduce.2
  952.1 22.3 reduce-scatter.44
  977.2 47.2 reduce-scatter.40
  1027.4 41.8 reduce-scatter.42
  1071.6 388.1 reduce-scatter.38
where the time goes:
time: 1560 us; the launch traced here: 1550 us
  waiting for transfers between devices  924 us (59%)
  blocking collectives  346 us (22%)
  other arithmetic  109 us (7%)
  local copies, waits for them, and re-layouts  76.5 us (5%)
  matrix products  64.4 us (4%)
  between operations  26.6 us (2%)
    reduce_scatter x1, waiting for transfers between devices, on_device(): lax.psum_scatter(totals[0][None], 'dp', scatter_dimension=1, tiled=True)  352 us
    reduce_scatter x8, waiting for transfers between devices, collect_rows(): return lax.psum_scatter(x, 'mp', scatter_dimension=0, tiled=True)  202 us
    all_gather x1, waiting for transfers between devices, on_device(): lax.all_gather(table.astype(jnp.bfloat16), 'dp', axis=1, tiled=True)  150 us
    all_gather x8, blocking collectives, spread_rows(): return lax.all_gather(x, 'mp', axis=0, tiled=True)  102 us
    unnamed x23, waiting for transfers between devices  96.5 us
    psum x1, blocking collectives, on_device(): g_norms = lax.psum(g_norms, ('dp', 'mp'))  77.3 us
    all_gather x1, blocking collectives, on_device(): lax.all_gather(w_mixed.astype(jnp.bfloat16), 'dp', axis=1, tiled=True)  50.5 us
    reduce_scatter x1, waiting for transfers between devices, on_device(): lax.psum_scatter(totals[3][None], 'dp', scatter_dimension=1, tiled=True)  48.2 us
  transfers between devices with their start and end apart: 20, of which 18 were waited for; matrix products, arithmetic and copies ran while one was open for 8% of the time, Pallas kernels for 0%

commit v1 on v0

--- a/solution.py
+++ b/solution.py
@@ -305,7 +305,18 @@
         )
         g_norms = g_norms + span_norms
         flat_ids = ids_span.reshape(-1)
-        d_rows = lax.all_gather(d_embedded, "mp", axis=0, tiled=True)
+        fan = lax.psum(1, "mp")
+        queue = []
+        for d in range(fan):
+            queue.append((d, (d + 1) % fan))
+        state_next = [None] * fan
+        state_next[fan - 1] = d_embedded
+        for c in range(fan - 2, -1, -1):
+            state_next[c] = lax.ppermute(state_next[c + 1], "mp", queue)
+        h_now = jnp.concatenate(state_next, 0)
+        local_out = lax.axis_index("mp")
+        part_next = (local_out + 1) * d_embedded.shape[0]
+        d_rows = jnp.roll(h_now, shift=part_next, axis=0)
         local_row, owned = vocab_place(flat_ids, weights[0].shape[0])
         g_table = (
             jnp.zeros(weights[0].shape, jnp.float32)

time: 1560 us -> 1490 us (0.955)
  waiting for transfers between devices: 924 us -> 846 us
    unnamed x23 -> x21, waiting for transfers between devices: 96.5 us -> 37.4 us
    ppermute x0 -> x6, waiting for transfers between devices: none -> 45.8 us  [on_device(): state_next[c] = lax.ppermute(state_next[c + 1], 'mp', queue)]
    all_gather x2 -> x0, waiting for transfers between devices: 35.4 us -> none  [on_device(): d_rows = lax.all_gather(d_embedded, 'mp', axis=0, tiled=True)]
    reduce_scatter x8, waiting for transfers between devices: 202 us -> 174 us  [collect_rows(): return lax.psum_scatter(x, 'mp', scatter_dimension=0, tiled=True)]
    unnamed x357 -> x369, local copies, waits for them, and re-layouts: 41.6 us -> 44.1 us
  transfers between devices with their start and end apart: 20 -> 24, of which waited for: 18 -> 21; matrix products, arithmetic and copies ran while one was open for 8% -> 9% of each run, Pallas kernels for 0% -> 0%
where the time goes in v1:
time: 1490 us; the launch traced here: 1480 us
  waiting for transfers between devices  846 us (57%)
  blocking collectives  345 us (23%)
  other arithmetic  112 us (8%)
  local copies, waits for them, and re-layouts  79 us (5%)
  matrix products  63.2 us (4%)
  between operations  26.7 us (2%)
    reduce_scatter x1, waiting for transfers between devices, on_device(): lax.psum_scatter(totals[0][None], 'dp', scatter_dimension=1, tiled=True)  352 us
    reduce_scatter x8, waiting for transfers between devices, collect_rows(): return lax.psum_scatter(x, 'mp', scatter_dimension=0, tiled=True)  174 us
    all_gather x1, waiting for transfers between devices, on_device(): lax.all_gather(table.astype(jnp.bfloat16), 'dp', axis=1, tiled=True)  150 us
    all_gather x8, blocking collectives, spread_rows(): return lax.all_gather(x, 'mp', axis=0, tiled=True)  102 us
    psum x1, blocking collectives, on_device(): g_norms = lax.psum(g_norms, ('dp', 'mp'))  77.2 us
    all_gather x1, blocking collectives, on_device(): lax.all_gather(w_mixed.astype(jnp.bfloat16), 'dp', axis=1, tiled=True)  50.5 us
    reduce_scatter x1, waiting for transfers between devices, on_device(): lax.psum_scatter(totals[3][None], 'dp', scatter_dimension=1, tiled=True)  48.2 us
    ppermute x6, waiting for transfers between devices, on_device(): state_next[c] = lax.ppermute(state_next[c + 1], 'mp', queue)  45.8 us
  transfers between devices with their start and end apart: 24, of which 21 were waited for; matrix products, arithmetic and copies ran while one was open for 9% of the time, Pallas kernels for 0%

profile of v1, /device:TPU:0, one launch (start us, length us, event | category | flops | bytes accessed | tf_op | source)
XLA Modules:
  0.0 1478.8 jit_solution(12203234582590836881)
XLA Ops:
  7.2 4.6 convert_element_type.165
  13.2 50.5 %all_gather.48 = bf16[1,768,3,192]{3,2,0,1:T(4,128)(2,1)S(1)} all-gather(bf16[1,192,3,192]{3,2,0,1:T(4,128)(2,1)S(1)} %copy.212), channel_id=1, replica_groups=mesh['enc'=2,'dp'=4,'mp'=4] {'dp'}, dimensions={1}, use_global_device_ids=true | all-gather | bytes 1105920 | tf_op jit(solution)/shard_map/all_gather | solution.py:249
  65.0 32.1 %all_gather.49 = bf16[1,192,768]{1,0,2:T(2,128)(2,1)S(1)} all-gather(bf16[1,192,192]{1,0,2:T(2,128)(2,1)S(1)} %copy.219), channel_id=1, replica_groups=mesh['enc'=2,'dp'=4,'mp'=4] {'dp'}, dimensions={2}, use_global_device_ids=true | all-gather | bytes 368640 | tf_op jit(solution)/shard_map/all_gather | solution.py:250
  97.7 150.2 %all-gather.4.cloned.1.call-done = bf16[1,7680,768]{2,1,0:T(8,128)(2,1)} async-done(((bf16[1,1920,768]{2,1,0:T(8,128)(2,1)}), bf16[1,7680,768]{2,1,0:T(8,128)(2,1)}) %all-gather.4.cloned.1.call-update) | async-done | bytes 11796496 | tf_op jit(solution)/shard_map/all_gather | solution.py:248
  248.0 8.3 gather_fusion
  259.4 8.4 gather_fusion.1
  268.9 14.0 reduce-scatter.19.cloned.1.call-done
  286.3 14.5 all_gather.47
  309.4 4.0 reduce-scatter.25.cloned.1.call-done
  316.1 31.6 %reduce-scatter.21.cloned.1.call-done = f32[128,768]{1,0:T(8,128)} async-done(((f32[512,768]{1,0:T(8,128)}), f32[128,768]{1,0:T(8,128)}) %reduce-scatter.21.cloned.1.call-update) | async-done | bytes 393232 | tf_op jit(solution)/shard_map/reduce_scatter | solution.py:31
  349.6 11.3 all_gather.53
  372.5 11.2 all_gather.50
  383.7 7.3 multiply_convert_fusion.3
  391.0 20.8 %all-gather.8.cloned.1.call-done = bf16[1,768,768]{1,2,0:T(8,128)(2,1)} async-done(((bf16[1,768,192]{1,2,0:T(8,128)(2,1)}), bf16[1,768,768]{1,2,0:T(8,128)(2,1)}) %all-gather.8.cloned.1.call-update) | async-done | bytes 1179664 | tf_op jit(solution)/shard_map/all_gather | solution.py:252
  411.8 3.5 fusion.47
  415.3 29.5 %reduce-scatter.27.cloned.1.call-done = f32[128,768]{1,0:T(8,128)} async-done(((f32[512,768]{1,0:T(8,128)}), f32[128,768]{1,0:T(8,128)}) %reduce-scatter.27.cloned.1.call-update) | async-done | bytes 393232 | tf_op jit(solution)/shard_map/reduce_scatter | solution.py:31
  448.0 31.4 %reduce-scatter.23.cloned.1.call-done = f32[128,768]{1,0:T(8,128)} async-done(((f32[512,768]{1,0:T(8,128)}), f32[128,768]{1,0:T(8,128)}) %reduce-scatter.23.cloned.1.call-update) | async-done | bytes 393232 | tf_op jit(solution)/shard_map/reduce_scatter | solution.py:31
  482.0 11.1 all_gather.54
  493.1 5.3 multiply_convert_fusion.2
  509.4 23.1 %reduce-scatter.29.cloned.1.call-done = f32[128,768]{1,0:T(8,128)} async-done(((f32[512,768]{1,0:T(8,128)}), f32[128,768]{1,0:T(8,128)}) %reduce-scatter.29.cloned.1.call-update) | async-done | bytes 393232 | tf_op jit(solution)/shard_map/reduce_scatter | solution.py:31
  535.6 16.5 %psum.21 = f32[8,768]{1,0:T(8,128)} all-reduce(f32[8,768]{1,0:T(8,128)} %pad_maximum_fusion), channel_id=1, replica_groups=mesh['enc'=2,'dp'=4,'mp'=4] {'mp'}, use_global_device_ids=true, to_apply=%region_22.23 | all-reduce | flops 6144 | bytes 49152 | tf_op jit(solution)/shard_map/psum | solution.py:271
  552.2 24.8 %all_gather.55 = f32[64,768]{1,0:T(8,128)S(1)} all-gather(f32[8,768]{1,0:T(8,128)} %psum.21), channel_id=1, replica_groups=mesh['enc'=2,'dp'=4,'mp'=4] {'enc','dp'}, dimensions={0}, use_global_device_ids=true | all-gather | bytes 221184 | tf_op jit(solution)/shard_map/all_gather | solution.py:272
  605.9 12.1 all_gather.58
  623.9 15.7 %all_gather.56 = bf16[512,768]{1,0:T(8,128)(2,1)S(1)} all-gather(bf16[128,768]{1,0:T(8,128)(2,1)S(1)} %add_convert_fusion.5), channel_id=1, replica_groups=mesh['enc'=2,'dp'=4,'mp'=4] {'mp'}, dimensions={0}, use_global_device_ids=true | all-gather | bytes 983040 | tf_op jit(solution)/shard_map/all_gather | solution.py:27
  639.6 3.3 add_convert_fusion.1
  645.8 8.6 reduce-scatter.35.cloned.1.call-done
  654.4 34.5 %reduce-scatter.31.cloned.1.call-done = f32[128,768]{1,0:T(8,128)} async-done(((f32[512,768]{1,0:T(8,128)}), f32[128,768]{1,0:T(8,128)}) %reduce-scatter.31.cloned.1.call-update) | async-done | bytes 393232 | tf_op jit(solution)/shard_map/reduce_scatter | solution.py:31
  695.9 11.1 all_gather.57
  716.0 14.9 %all_gather.59 = bf16[512,768]{1,0:T(8,128)(2,1)S(1)} all-gather(bf16[128,768]{1,0:T(8,128)(2,1)S(1)} %add_convert_fusion.2), channel_id=1, replica_groups=mesh['enc'=2,'dp'=4,'mp'=4] {'mp'}, dimensions={0}, use_global_device_ids=true | all-gather | bytes 983040 | tf_op jit(solution)/shard_map/all_gather | solution.py:27
  742.5 4.3 copy.238
  761.5 3.0 copy.258
  767.5 15.1 %reduce-scatter.37.cloned.1.call-done = f32[128,768]{1,0:T(8,128)} async-done(((f32[512,768]{1,0:T(8,128)}), f32[128,768]{1,0:T(8,128)}) %reduce-scatter.37.cloned.1.call-update) | async-done | bytes 393232 | tf_op jit(solution)/shard_map/reduce_scatter | solution.py:31
  788.4 10.0 collective-permute-done
  799.0 7.9 collective-permute-done.3
  807.4 7.9 collective-permute-done.1
  815.8 7.9 collective-permute-done.4
  824.5 7.8 collective-permute-done.2
  835.2 4.3 collective-permute-done.5
  842.5 17.2 %scatter_custom_fusion.1 = f32[7680,768]{1,0:T(8,128)} fusion(s32[1024]{0:T(1024)S(1)} %bitcast.302, f32[]{:T(128)} %constant.353.clone.1, f32[512,768]{1,0:T(8,128)S(1)} %fusion.12, f32[]{:T(128)} %constant.360.clone.1, f32[512,768]{1,0:T(8,128)S(1)} %fusion.20), kind=kCustom, calls=%fused_computation.5 | custom fusion | flops 1572864 | bytes 26738696 | tf_op jit(solution)/shard_map/add | solution.py:328
  864.8 16.3 %all-reduce.3.cloned.1.call-done = f32[1,768,768]{1,0,2:T(1,128)} async-done(((f32[1,768,768]{1,0,2:T(1,128)}), f32[1,768,768]{1,0,2:T(1,128)}) %all-reduce.3.cloned.1.call-update) | async-done | bytes 2359312
  881.1 3.6 multiply_reduce_fusion.3
  884.8 20.8 %reduce-scatter.45.cloned.1.call-done = f32[192,192]{1,0:T(8,128)} async-done(((f32[768,192]{1,0:T(8,128)}), f32[192,192]{1,0:T(8,128)}) %reduce-scatter.45.cloned.1.call-update) | async-done | bytes 147472
  907.4 48.2 %reduce-scatter.41.cloned.1.call-done = f32[1,192,768]{2,1,0:T(8,128)} async-done(((f32[1,768,768]{2,1,0:T(8,128)}), f32[1,192,768]{2,1,0:T(8,128)}) %reduce-scatter.41.cloned.1.call-update) | async-done | bytes 589840 | tf_op jit(solution)/shard_map/reduce_scatter | solution.py:334
  957.6 77.2 %psum.22 = f32[6,768]{1,0:T(8,128)S(1)} all-reduce(f32[6,768]{1,0:T(8,128)S(1)} %add.672), channel_id=1, replica_groups=mesh['enc'=2,'dp'=4,'mp'=4] {'dp','mp'}, use_global_device_ids=true, to_apply=%region_60.61 | all-reduce | flops 4608 | bytes 36864 | tf_op jit(solution)/shard_map/psum | solution.py:337
  1038.6 352.1 %reduce-scatter.39.cloned.1.call-done = f32[1,1920,768]{2,1,0:T(8,128)} async-done(((f32[1,7680,768]{2,1,0:T(8,128)}), f32[1,1920,768]{2,1,0:T(8,128)}) %reduce-scatter.39.cloned.1.call-update) | async-done | bytes 5898256 | tf_op jit(solution)/shard_map/reduce_scatter | solution.py:331
  1390.7 4.8 multiply_reduce_fusion
  1399.4 42.3 %psum.23 = f32[]{:T(128)} all-reduce(f32[]{:T(128)S(6)} %add.683), channel_id=1, replica_groups=mesh['enc'=2,'dp'=4,'mp'=4] {'enc','dp','mp'}, use_global_device_ids=true, to_apply=%region_77.79 | all-reduce | flops 1 | bytes 8 | tf_op jit(solution)/shard_map/psum | solution.py:342
  1456.6 12.6 multiply_subtract_fusion
  (603 shorter events, 174.6 us)
Async XLA Ops:
  7.2 240.8 %all-gather.4.cloned.1.call-start = ((), (), s32[]{:S(2)}) async-start(), calls=%async_computation.14 | async-start | bytes 14745600 | tf_op jit(solution)/shard_map/all_gather | solution.py:248
  11.8 271.1 %reduce-scatter.19.cloned.1.call-start = ((), (), s32[]{:S(2)}) async-start(), calls=%async_computation.15 | async-start | bytes 983040 | tf_op jit(solution)/shard_map/reduce_scatter | solution.py:76
  64.5 296.3 %copy-start.8 = (bf16[1,768,3,192]{1,3,2,0:T(8,128)(2,1)}, bf16[1,768,3,192]{1,3,2,0:T(8,128)(2,1)S(1)}, u32[]{:S(2)}) copy-start(bf16[1,768,3,192]{1,3,2,0:T(8,128)(2,1)S(1)} %copy.213) | copy-start | bytes 2654212
  97.6 207.4 %copy-start.10 = (bf16[1,192,768]{2,1,0:T(8,128)(2,1)}, bf16[1,192,768]{2,1,0:T(8,128)(2,1)S(1)}, u32[]{:S(2)}) copy-start(bf16[1,192,768]{2,1,0:T(8,128)(2,1)S(1)} %copy.220) | copy-start | bytes 884740
  97.7 158.6 %copy-start.94 = (s32[512,1]{0,1:T(1,128)}, s32[512,1]{0,1:T(1,128)S(1)}, u32[]{:S(2)}) copy-start(s32[512,1]{0,1:T(1,128)S(1)} %get-tuple-element.259) | copy-start | bytes 6148
  97.7 159.8 %copy-start.92 = (s32[512,1]{0,1:T(1,128)}, s32[512,1]{0,1:T(1,128)S(1)}, u32[]{:S(2)}) copy-start(s32[512,1]{0,1:T(1,128)S(1)} %get-tuple-element.258) | copy-start | bytes 6148
  97.7 158.5 %copy-start.133 = (pred[512]{0:T(512)(128)(4,1)}, pred[512]{0:T(512)(128)(4,1)S(1)}, u32[]{:S(2)}) copy-start(pred[512]{0:T(512)(128)(4,1)S(1)} %fusion.158) | copy-start | bytes 1540
  257.4 56.0 %reduce-scatter.25.cloned.1.call-start = ((), (), s32[]{:S(2)}) async-start(), calls=%async_computation.20 | async-start | bytes 983040 | tf_op jit(solution)/shard_map/reduce_scatter | solution.py:76
  258.3 221.1 %copy-start.86 = (f32[768]{0:T(1024)}, f32[768]{0:T(1024)S(1)}, u32[]{:S(2)}) copy-start(f32[768]{0:T(1024)S(1)} %get-tuple-element.140) | copy-start | bytes 9220
  258.3 274.1 %copy-start.80 = (f32[768]{0:T(1024)}, f32[768]{0:T(1024)S(1)}, u32[]{:S(2)}) copy-start(f32[768]{0:T(1024)S(1)} %get-tuple-element.141) | copy-start | bytes 9220
  258.3 276.2 %copy-start.82 = (f32[768]{0:T(1024)}, f32[768]{0:T(1024)S(1)}, u32[]{:S(2)}) copy-start(f32[768]{0:T(1024)S(1)} %get-tuple-element.139) | copy-start | bytes 9220
  268.9 78.8 %reduce-scatter.21.cloned.1.call-start = ((), (), s32[]{:S(2)}) async-start(), calls=%async_computation.16 | async-start | bytes 1966080 | tf_op jit(solution)/shard_map/reduce_scatter | solution.py:31
  306.5 41.2 %copy-start.5 = (bf16[128,768]{1,0:T(8,128)(2,1)S(1)}, bf16[128,768]{1,0:T(8,128)(2,1)}, u32[]{:S(2)}) copy-start(bf16[128,768]{1,0:T(8,128)(2,1)} %reduce-scatter.19.cloned.1.call-done) | copy-start | bytes 589828
  306.5 77.2 %all-gather.6.cloned.1.call-start = ((), (), s32[]{:S(2)}) async-start(), calls=%async_computation.17 | async-start | bytes 1474560 | tf_op jit(solution)/shard_map/all_gather | solution.py:251
  308.5 103.3 %all-gather.8.cloned.1.call-start = ((), (), s32[]{:S(2)}) async-start(), calls=%async_computation.18 | async-start | bytes 1474560 | tf_op jit(solution)/shard_map/all_gather | solution.py:252
  309.3 135.5 %reduce-scatter.27.cloned.1.call-start = ((), (), s32[]{:S(2)}) async-start(), calls=%async_computation.21 | async-start | bytes 1966080 | tf_op jit(solution)/shard_map/reduce_scatter | solution.py:31
  314.4 48.8 %copy-start.98 = (f32[128]{0:T(128)}, f32[128]{0:T(128)S(1)}, u32[]{:S(2)}) copy-start(f32[128]{0:T(128)S(1)} %broadcast_multiply_fusion.2) | copy-start | bytes 1540
  316.1 47.2 %copy-start.126 = (f32[128]{0:T(128)}, f32[128]{0:T(128)S(1)}, u32[]{:S(2)}) copy-start(f32[128]{0:T(128)S(1)} %fusion.172) | copy-start | bytes 1540
  370.9 108.5 %reduce-scatter.23.cloned.1.call-start = ((), (), s32[]{:S(2)}) async-start(), calls=%async_computation.19 | async-start | bytes 1966080 | tf_op jit(solution)/shard_map/reduce_scatter | solution.py:31
  415.3 117.2 %reduce-scatter.29.cloned.1.call-start = ((), (), s32[]{:S(2)}) async-start(), calls=%async_computation.22 | async-start | bytes 1966080 | tf_op jit(solution)/shard_map/reduce_scatter | solution.py:31
  501.4 153.0 %reduce-scatter.35.cloned.1.call-start = ((), (), s32[]{:S(2)}) async-start(), calls=%async_computation.25 | async-start | bytes 1966080 | tf_op jit(solution)/shard_map/reduce_scatter | solution.py:31
  533.8 46.5 %copy-start.122 = (f32[128]{0:T(128)}, f32[128]{0:T(128)S(1)}, u32[]{:S(2)}) copy-start(f32[128]{0:T(128)S(1)} %broadcast_multiply_fusion) | copy-start | bytes 1540
  622.1 66.8 %reduce-scatter.31.cloned.1.call-start = ((), (), s32[]{:S(2)}) async-start(), calls=%async_computation.23 | async-start | bytes 1966080 | tf_op jit(solution)/shard_map/reduce_scatter | solution.py:31
  645.7 43.2 %copy-start.81 = (f32[768]{0:T(1024)S(1)}, f32[768]{0:T(1024)}, u32[]{:S(2)}) copy-start(f32[768]{0:T(1024)} %copy-done.80) | copy-start | bytes 9220
  645.7 43.2 %copy-start.114 = (f32[128]{0:T(128)S(1)}, f32[128]{0:T(128)}, u32[]{:S(2)}) copy-start(f32[128]{0:T(128)} %copy-done.113) | copy-start | bytes 1540
  645.8 43.2 %copy-start.116 = (f32[128]{0:T(128)S(1)}, f32[128]{0:T(128)}, u32[]{:S(2)}) copy-start(f32[128]{0:T(128)} %copy-done.115) | copy-start | bytes 1540
  645.8 121.7 %reduce-scatter.33.cloned.1.call-start = ((), (), s32[]{:S(2)}) async-start(), calls=%async_computation.24 | async-start | bytes 1966080 | tf_op jit(solution)/shard_map/reduce_scatter | solution.py:31
  715.6 67.0 %reduce-scatter.37.cloned.1.call-start = ((), (), s32[]{:S(2)}) async-start(), calls=%async_computation.26 | async-start | bytes 1966080 | tf_op jit(solution)/shard_map/reduce_scatter | solution.py:31
  739.0 142.1 %all-reduce.3.cloned.1.call-start = ((), (), s32[]{:S(2)}) async-start(), calls=%async_computation.31 | async-start | bytes 4718592
  746.8 158.7 %reduce-scatter.45.cloned.1.call-start = ((), (), s32[]{:S(2)}) async-start(), calls=%async_computation.30 | async-start | bytes 983040
  752.7 202.9 %reduce-scatter.41.cloned.1.call-start = ((), (), s32[]{:S(2)}) async-start(), calls=%async_computation.28 | async-start | bytes 2949120 | tf_op jit(solution)/shard_map/reduce_scatter | solution.py:334
  757.1 279.0 %reduce-scatter.43.cloned.1.call-start = ((), (), s32[]{:S(2)}) async-start(), calls=%async_computation.29 | async-start | bytes 2457600
  767.4 623.3 %reduce-scatter.39.cloned.1.call-start = ((), (), s32[]{:S(2)}) async-start(), calls=%async_computation.27 | async-start | bytes 29491200 | tf_op jit(solution)/shard_map/reduce_scatter | solution.py:331
  784.2 40.3 %copy-start.93 = (s32[512,1]{0,1:T(1,128)S(1)}, s32[512,1]{0,1:T(1,128)}, u32[]{:S(2)}) copy-start(s32[512,1]{0,1:T(1,128)} %copy-done.92) | copy-start | bytes 6148
  784.2 40.3 %copy-start.95 = (s32[512,1]{0,1:T(1,128)S(1)}, s32[512,1]{0,1:T(1,128)}, u32[]{:S(2)}) copy-start(s32[512,1]{0,1:T(1,128)} %copy-done.94) | copy-start | bytes 6148
  785.5 13.0 collective-permute-start
  787.0 19.9 %collective-permute-start.3 = (f32[128,768]{1,0:T(8,128)S(1)}, f32[128,768]{1,0:T(8,128)S(1)}, u32[]{:S(2)}, u32[]{:S(2)}) collective-permute-start(f32[128,768]{1,0:T(8,128)S(1)} %get-tuple-element.215), channel_id=1, source_target_pairs={{0,1},{1,2},{2,3},{3,0},{4,5},{5,6},{6,7},{7,4},{8,9},{9,10},{10,1... | collective-permute-start | bytes 1179656 | tf_op jit(solution)/shard_map/ppermute | solution.py:315
  798.5 16.9 %collective-permute-start.1 = (f32[128,768]{1,0:T(8,128)S(1)}, f32[128,768]{1,0:T(8,128)S(1)}, u32[]{:S(2)}, u32[]{:S(2)}) collective-permute-start(f32[128,768]{1,0:T(8,128)S(1)} %collective-permute-done), channel_id=1, source_target_pairs={{0,1},{1,2},{2,3},{3,0},{4,5},{5,6},{6,7},{7,4},{8,9},{9,10},{10,1... | collective-permute-start | bytes 1179656 | tf_op jit(solution)/shard_map/ppermute | solution.py:315
  806.9 28.3 %copy-start.73 = (f32[128,768]{1,0:T(8,128)}, f32[128,768]{1,0:T(8,128)S(1)}, u32[]{:S(2)}) copy-start(f32[128,768]{1,0:T(8,128)S(1)} %collective-permute-done.3) | copy-start | bytes 1179652
  806.9 16.9 %collective-permute-start.4 = (f32[128,768]{1,0:T(8,128)S(1)}, f32[128,768]{1,0:T(8,128)S(1)}, u32[]{:S(2)}, u32[]{:S(2)}) collective-permute-start(f32[128,768]{1,0:T(8,128)S(1)} %collective-permute-done.3), channel_id=1, source_target_pairs={{0,1},{1,2},{2,3},{3,0},{4,5},{5,6},{6,7},{7,4},{8,9},{9,10},{10,1... | collective-permute-start | bytes 1179656 | tf_op jit(solution)/shard_map/ppermute | solution.py:315
  815.3 17.0 %collective-permute-start.2 = (f32[128,768]{1,0:T(8,128)S(1)}, f32[128,768]{1,0:T(8,128)}, u32[]{:S(2)}, u32[]{:S(2)}) collective-permute-start(f32[128,768]{1,0:T(8,128)S(1)} %collective-permute-done.1), channel_id=1, source_target_pairs={{0,1},{1,2},{2,3},{3,0},{4,5},{5,6},{6,7},{7,4},{8,9},{9,10},{10,1... | collective-permute-start | bytes 1179656 | tf_op jit(solution)/shard_map/ppermute | solution.py:315
  823.7 15.8 %collective-permute-start.5 = (f32[128,768]{1,0:T(8,128)S(1)}, f32[128,768]{1,0:T(8,128)}, u32[]{:S(2)}, u32[]{:S(2)}) collective-permute-start(f32[128,768]{1,0:T(8,128)S(1)} %collective-permute-done.4), channel_id=1, source_target_pairs={{0,1},{1,2},{2,3},{3,0},{4,5},{5,6},{6,7},{7,4},{8,9},{9,10},{10,1... | collective-permute-start | bytes 1179656 | tf_op jit(solution)/shard_map/ppermute | solution.py:315
  863.4 94.1 %copy-start.111 = (f32[768]{0:T(1024)S(1)}, f32[768]{0:T(1024)}, u32[]{:S(2)}) copy-start(f32[768]{0:T(1024)} %get-tuple-element.148) | copy-start | bytes 9220
  863.4 94.1 %copy-start.110 = (f32[768]{0:T(1024)S(1)}, f32[768]{0:T(1024)}, u32[]{:S(2)}) copy-start(f32[768]{0:T(1024)} %get-tuple-element.147) | copy-start | bytes 9220
  863.4 94.1 %copy-start.109 = (f32[768]{0:T(1024)S(1)}, f32[768]{0:T(1024)}, u32[]{:S(2)}) copy-start(f32[768]{0:T(1024)} %get-tuple-element.130) | copy-start | bytes 9220
  863.4 94.1 %copy-start.108 = (f32[768]{0:T(1024)S(1)}, f32[768]{0:T(1024)}, u32[]{:S(2)}) copy-start(f32[768]{0:T(1024)} %get-tuple-element.133) | copy-start | bytes 9220
  906.8 130.8 %copy-start.46 = (f32[1,192,192]{2,1,0:T(8,128)}, f32[1,192,192]{2,1,0:T(8,128)S(1)}, u32[]{:S(2)}) copy-start(f32[1,192,192]{2,1,0:T(8,128)S(1)} %copy.261) | copy-start | bytes 442372
  1038.6 403.9 %copy-start.91 = (f32[1,6,768]{2,0,1:T(1,128)S(1)}, f32[1,6,768]{2,0,1:T(1,128)}, u32[]{:S(2)}) copy-start(f32[1,6,768]{2,0,1:T(1,128)} %param.48) | copy-start | bytes 55300
  (146 other events, 919.2 us)
Sparse Core Ops, SparseCore 0:
  11.9 235.9 all-gather.3
  257.5 25.3 reduce-scatter.18
  286.4 26.9 reduce-scatter.24
  316.8 30.8 reduce-scatter.20
  349.7 30.4 all-gather.5
  382.2 29.5 all-gather.7
  414.8 30.0 reduce-scatter.26
  448.4 30.9 reduce-scatter.22
  501.5 30.9 reduce-scatter.28
  622.3 32.0 reduce-scatter.34
  658.0 30.8 reduce-scatter.30
  715.7 32.9 reduce-scatter.32
  751.7 30.8 reduce-scatter.36
  785.4 95.6 all-reduce.2
  883.2 22.3 reduce-scatter.44
  908.3 47.2 reduce-scatter.40
  958.4 41.9 reduce-scatter.42
  1002.6 388.0 reduce-scatter.38
